TPU v7x, 32 devices: a whole 2x2x4 slice. The times are simulated.
32 devices in a mesh: groups: 2 (over y), ctx: 4 (over z), dp: 4 (over x, core).
Axes of the slice: x: 2, y: 2, z: 4, core: 2. Of those that a mesh axis runs over, the one named last changes fastest.
Arguments:
- tokens: int32 [8, 1024, 128], P(('groups', 'dp'), 'ctx'), parts along dimension 0, may hold values from 0 to 3
- targets: int32 [8, 1024, 896], P(('groups', 'dp'), 'ctx'), parts along dimension 0, may hold values from 0 to 3
- stem_half: bfloat16 [1024, 384], P('groups'), parts along dimension 0, may hold values from -0.5 to 0.5
- conv_half: bfloat16 [10, 768, 256], P('groups'), parts along dimension 0, may hold values from -0.09375 to 0.09375
- point_half: bfloat16 [1024, 384], P('groups'), parts along dimension 0, may hold values from -0.25 to 0.25
- head_half: bfloat16 [768, 896], P('groups'), parts along dimension 0, may hold values from -0.21875 to 0.21875
Outputs:
- grad_stem: float32 [1024, 384], P(('groups', 'ctx', 'dp')), parts along dimension 0
- grad_conv: float32 [7680, 256], P(('groups', 'ctx', 'dp')), parts along dimension 0
- grad_point: float32 [1024, 384], P(('groups', 'ctx', 'dp')), parts along dimension 0
- grad_head: float32 [1792, 384], P(('groups', 'ctx', 'dp')), parts along dimension 0
There are 2 independent parts, one for each index of `groups`. A program takes and returns all parts, laid end to end along the dimension named above; each array names one. Nothing has to cross between parts.
All inputs are finite; a program needn't handle non-finite values.
Results may differ from a plain program's by a relative error of at most 0.00095.
Values may be sent and summed in bfloat16 or wider, within the bound.
A program may use at most 64 MiB of HBM per device.

v0:
```python
import math

import jax
import jax.numpy as jnp
from jax import lax
from jax.sharding import PartitionSpec as P

DILATION_STEP = 128


def with_halo(x, sides, width):
    for axis, dim in sides:
        count, length = (lax.axis_size(axis), x.shape[dim])
        up = [(i, (i + 1) % count) for i in range(count - 1)]
        down = [(j, i) for i, j in up]
        last = lax.slice_in_dim(x, length - width, length, axis=dim)
        leading = lax.slice_in_dim(x, 0, width, axis=dim)
        before = lax.ppermute(last, axis, up)
        after = lax.ppermute(leading, axis, down)
        x = jnp.concatenate([before, x, after], axis=dim)
    return x


def expand_weights(stem_half, conv_half, point_half, head_half):
    stem_full = jnp.concatenate([stem_half, stem_half[::-1, ::-1]], axis=1)
    conv_full = jnp.concatenate([conv_half, conv_half[::-1, ::-1, ::-1]], axis=2)
    point_full = jnp.concatenate([point_half, point_half[::-1, ::-1]], axis=1)
    head_full = jnp.concatenate([head_half, head_half[::-1, :]], axis=0)
    return (stem_full, conv_full, point_full, head_full)


def gelu_slope(values):
    normal_cdf = 0.5 * (1.0 + lax.erf(values * (1.0 / math.sqrt(2.0))))
    normal_pdf = jnp.exp(-0.5 * values * values) * (1.0 / math.sqrt(2.0 * math.pi))
    return normal_cdf + values * normal_pdf


def regroup_rows(term, outer_count, inner_count):
    block_rows = term.shape[0] // (outer_count * inner_count)
    shaped = term.reshape(outer_count, inner_count, block_rows, term.shape[1])
    return jnp.swapaxes(shaped, 0, 1).reshape(term.shape)


def local(tokens, targets, stem_half, conv_half, point_half, head_half):
    stem_full, conv_full, point_full, head_full = expand_weights(
        stem_half, conv_half, point_half, head_half
    )
    sequence_total, sequence_length, base_count = tokens.shape
    total_rows = sequence_total * sequence_length
    kernel_taps = conv_full.shape[0]
    channel_total = stem_full.shape[1]
    inner_features = conv_full.shape[2]
    ctx_count = lax.axis_size("ctx")
    dp_count = lax.axis_size("dp")
    scale = 1.0 / math.sqrt(total_rows * ctx_count * dp_count)
    onehot = (
        (tokens[..., None] == jnp.arange(4, dtype=jnp.int32))
        .astype(jnp.bfloat16)
        .reshape(total_rows, 4 * base_count)
    )
    embed = jnp.dot(onehot, stem_full, preferred_element_type=jnp.float32).astype(jnp.bfloat16)
    embed_wide = embed.astype(jnp.float32)
    inv_root = lax.rsqrt(jnp.mean(embed_wide * embed_wide, axis=1, keepdims=True) + 1e-05)
    normed_input = (embed_wide * inv_root).astype(jnp.bfloat16)
    padded_input = with_halo(
        normed_input.reshape(sequence_total, sequence_length, channel_total),
        (("ctx", 1),),
        2 * DILATION_STEP,
    )
    pre = jnp.zeros((total_rows, inner_features), jnp.float32)
    windows = []
    for kernel_tap_index in range(kernel_taps):
        sliding_window = padded_input[
            :, kernel_tap_index * DILATION_STEP : kernel_tap_index * DILATION_STEP + sequence_length
        ].reshape(total_rows, channel_total)
        windows.append(sliding_window)
        pre = pre + jnp.dot(
            sliding_window, conv_full[kernel_tap_index], preferred_element_type=jnp.float32
        )
    activated = jax.nn.gelu(pre, approximate=False).astype(jnp.bfloat16)
    after = (
        embed_wide + jnp.dot(activated, point_full, preferred_element_type=jnp.float32)
    ).astype(jnp.bfloat16)
    logits = jnp.dot(after, head_full, preferred_element_type=jnp.float32)
    counts = targets.reshape(total_rows, -1).astype(jnp.float32)
    loss_grad = ((jnp.exp(logits) - counts) * scale).astype(jnp.bfloat16)
    half_c = channel_total // 2
    head_sum = jnp.dot(loss_grad.T, after, preferred_element_type=jnp.float32)
    head_term = head_sum[:, :half_c] + head_sum[:, half_c:][:, ::-1]
    up_grad = jnp.dot(loss_grad, head_full.T, preferred_element_type=jnp.float32).astype(
        jnp.bfloat16
    )
    point_sum = jnp.dot(activated.T, up_grad, preferred_element_type=jnp.float32)
    point_term = point_sum[:, :half_c] + point_sum[:, half_c:][::-1, ::-1]
    act_grad = jnp.dot(up_grad, point_full.T, preferred_element_type=jnp.float32)
    preactivation_gradient = (act_grad * gelu_slope(pre)).astype(jnp.bfloat16)
    conv_sum = jnp.stack(
        [
            jnp.dot(
                windows[kernel_tap_index].T,
                preactivation_gradient,
                preferred_element_type=jnp.float32,
            )
            for kernel_tap_index in range(kernel_taps)
        ]
    )
    half_h = inner_features // 2
    conv_term = (conv_sum[..., :half_h] + conv_sum[..., half_h:][::-1, ::-1, ::-1]).reshape(
        kernel_taps * channel_total, half_h
    )
    padded_gradient = with_halo(
        preactivation_gradient.reshape(sequence_total, sequence_length, inner_features),
        (("ctx", 1),),
        2 * DILATION_STEP,
    )
    normed_grad = jnp.zeros((total_rows, channel_total), jnp.float32)
    for kernel_tap_index in range(kernel_taps):
        offset_begin = (kernel_taps - 1 - kernel_tap_index) * DILATION_STEP
        piece = padded_gradient[:, offset_begin : offset_begin + sequence_length].reshape(
            total_rows, inner_features
        )
        normed_grad = normed_grad + jnp.dot(
            piece, conv_full[kernel_tap_index].T, preferred_element_type=jnp.float32
        )
    inner_mean = jnp.mean(normed_grad * embed_wide, axis=1, keepdims=True)
    embed_grad = (
        inv_root * normed_grad
        - embed_wide * inv_root * inv_root * inv_root * inner_mean
        + up_grad.astype(jnp.float32)
    ).astype(jnp.bfloat16)
    stem_sum = jnp.dot(onehot.T, embed_grad, preferred_element_type=jnp.float32)
    stem_term = stem_sum[:, :half_c] + stem_sum[:, half_c:][::-1, ::-1]
    stem_moved = regroup_rows(stem_term, ctx_count, dp_count)
    conv_moved = regroup_rows(conv_term, ctx_count, dp_count)
    point_moved = regroup_rows(point_term, ctx_count, dp_count)
    head_moved = regroup_rows(head_term, ctx_count, dp_count)
    first = (
        lax.psum_scatter(stem_moved, "dp", scatter_dimension=0, tiled=True),
        lax.psum_scatter(conv_moved, "dp", scatter_dimension=0, tiled=True),
        lax.psum_scatter(point_moved, "dp", scatter_dimension=0, tiled=True),
        lax.psum_scatter(head_moved, "dp", scatter_dimension=0, tiled=True),
    )
    summed = (
        lax.psum_scatter(first[0], "ctx", scatter_dimension=0, tiled=True),
        lax.psum_scatter(first[1], "ctx", scatter_dimension=0, tiled=True),
        lax.psum_scatter(first[2], "ctx", scatter_dimension=0, tiled=True),
        lax.psum_scatter(first[3], "ctx", scatter_dimension=0, tiled=True),
    )
    return (summed[0], summed[1], summed[2], summed[3])


def solution(mesh):
    return jax.shard_map(
        local,
        mesh=mesh,
        in_specs=(
            P(("groups", "dp"), "ctx", None),
            P(("groups", "dp"), "ctx", None),
            P("groups", None),
            P("groups", None, None),
            P("groups", None),
            P("groups", None),
        ),
        out_specs=(
            P(("groups", "ctx", "dp"), None),
            P(("groups", "ctx", "dp"), None),
            P(("groups", "ctx", "dp"), None),
            P(("groups", "ctx", "dp"), None),
        ),
        check_vma=False,
    )
```

profile of v0, /device:TPU:0, one launch (start us, length us, event | category | flops | bytes accessed | tf_op | source)
XLA Modules:
  0.0 308.4 jit_solution(17623176389302653654)
XLA Ops:
  7.3 1.0 copy.19
  8.4 0.2 eq.26
  8.6 1.3 rev.24
  10.0 0.1 broadcast_compare_fusion
  10.2 0.5 fusion.15
  10.7 0.9 fusion.86
  11.6 1.3 collective-permute-start.1
  12.8 6.3 %collective-permute-start = (bf16[1,256,768]{2,1,0:T(8,128)(2,1)}, bf16[1,256,768]{2,1,0:T(8,128)(2,1)}, u32[]{:S(2)}, u32[]{:S(2)}) collective-permute-start(bf16[1,256,768]{2,1,0:T(8,128)(2,1)} %fusion.86), channel_id=1, source_target_pairs={{0,4},{4,8},{8,12},{1,5},{5,9},{9,13},{2,6},{6,10},{10,14},{3,7},{... | collective-permute-start | bytes 1179656 | tf_op jit(solution)/shard_map/ppermute | solution.py:18
  19.2 6.7 %rev.26 = bf16[512,384]{1,0:T(8,128)(2,1)} reverse(bf16[512,384]{1,0:T(8,128)(2,1)} %param.10), dimensions={0,1} | reverse | bytes 786432 | tf_op jit(solution)/shard_map/rev | solution.py:27
  25.9 7.0 %rev.27 = bf16[384,896]{1,0:T(8,128)(2,1)} reverse(bf16[384,896]{1,0:T(8,128)(2,1)S(1)} %copy-done.8), dimensions={0} | reverse | bytes 1376256 | tf_op jit(solution)/shard_map/rev | solution.py:28
  32.9 21.2 %rev.25 = bf16[5,768,256]{2,1,0:T(8,128)(2,1)} reverse(bf16[5,768,256]{2,1,0:T(8,128)(2,1)S(1)} %copy-done), dimensions={0,1,2} | reverse | bytes 3932160 | tf_op jit(solution)/shard_map/rev | solution.py:26
  54.1 1.4 fusion.24
  55.5 0.4 fusion.84
  55.9 1.4 fusion.68
  57.4 1.4 fusion.6
  58.8 1.4 fusion.51
  60.1 2.6 fusion.31
  62.8 0.4 fusion.5
  63.1 0.7 copy-done.12
  64.0 0.4 copy-done.16
  64.4 0.6 fusion.4
  65.1 0.6 convolution_convert_fusion
  65.7 0.5 fusion.37
  66.2 3.9 %collective-permute-start.3 = (bf16[1,256,512]{2,1,0:T(8,128)(2,1)S(1)}, bf16[1,256,512]{2,1,0:T(8,128)(2,1)}, u32[]{:S(2)}, u32[]{:S(2)}) collective-permute-start(bf16[1,256,512]{2,1,0:T(8,128)(2,1)S(1)} %bitcast.109), channel_id=1, source_target_pairs={{0,4},{4,8},{8,12},{1,5},{5,9},{9,13},{2,6},{6,10},{10,14},{3,7},{... | collective-permute-start | bytes 786440 | tf_op jit(solution)/shard_map/ppermute | solution.py:18
  70.1 1.3 collective-permute-start.2
  71.4 0.4 fusion.94
  71.8 1.2 copy-done.5
  73.0 1.0 slice.90
  73.9 7.2 %rev.30 = f32[512,384]{1,0:T(8,128)} reverse(f32[512,384]{1,0:T(8,128)} %slice.90), dimensions={0,1} | reverse | bytes 1572864 | tf_op jit(solution)/shard_map/rev | solution.py:94
  81.1 1.5 slice_add_fusion.2
  82.6 0.9 copy.22
  83.6 1.7 fusion.93
  85.3 1.3 fusion.64
  86.7 1.3 fusion.61
  88.0 1.4 fusion.3
  89.3 1.5 fusion.16
  90.8 0.6 fusion.46
  91.5 4.5 %rev.28 = f32[512,384]{1,0:T(8,128)} reverse(f32[512,384]{1,0:T(8,128)S(1)} %slice.86), dimensions={0,1} | reverse | bytes 1572864 | tf_op jit(solution)/shard_map/rev | solution.py:132
  96.0 1.2 slice_add_fusion.3
  97.2 1.0 copy.20
  98.3 1.7 fusion.95
  100.0 1.2 slice.92
  101.2 11.9 %rev.31 = f32[896,384]{1,0:T(8,128)} reverse(f32[896,384]{1,0:T(8,128)} %slice.92), dimensions={1} | reverse | bytes 2752512 | tf_op jit(solution)/shard_map/rev | solution.py:89
  113.1 1.5 slice_add_fusion.1
  114.5 1.2 copy.23
  115.7 0.2 reduce-scatter.15.cloned.1.call-start
  116.0 1.4 bitcast_dynamic-update-slice_fusion.4
  117.4 1.5 bitcast_dynamic-update-slice_fusion.3
  118.8 0.5 bitcast_dynamic-update-slice_fusion.2
  119.3 1.4 bitcast_dynamic-update-slice_fusion.1
  120.7 1.4 bitcast_dynamic-update-slice_fusion
  122.1 3.0 copy-done.3
  125.2 2.4 slice.88
  127.6 32.1 %rev.29 = f32[5,768,256]{2,1,0:T(8,128)} reverse(f32[5,768,256]{2,1,0:T(8,128)} %slice.88), dimensions={0,1,2} | reverse | bytes 7864320 | tf_op jit(solution)/shard_map/rev | solution.py:108
  159.7 3.9 %slice_add_fusion = f32[5,768,256]{2,1,0:T(8,128)S(1)} fusion(f32[5,768,256]{2,1,0:T(8,128)} %rev.29, f32[5,768,512]{2,1,0:T(8,128)} %copy-done.3), kind=kLoop, calls=%fused_computation.8 | loop fusion | flops 983040 | bytes 11796480 | tf_op jit(solution)/shard_map/add | solution.py:108
  163.6 2.2 copy.21
  165.9 0.5 reduce-scatter.21.cloned.1.call-update
  166.5 0.5 reduce-scatter.13.cloned.1.call-update
  167.1 0.7 reduce-scatter.25.cloned.1.call-update
  167.8 42.6 %reduce-scatter.15.cloned.1.call-done = f32[960,256]{1,0:T(8,128)} async-done(((f32[3840,256]{1,0:T(8,128)}), f32[960,256]{1,0:T(8,128)}) %reduce-scatter.15.cloned.1.call-update) | async-done | bytes 983056 | tf_op jit(solution)/shard_map/reduce_scatter | solution.py:139
  210.4 22.1 %reduce-scatter.21.cloned.1.call-done = f32[32,384]{1,0:T(8,128)} async-done(((f32[128,384]{1,0:T(8,128)}), f32[32,384]{1,0:T(8,128)}) %reduce-scatter.21.cloned.1.call-update) | async-done | bytes 49168 | tf_op jit(solution)/shard_map/reduce_scatter | solution.py:146
  232.4 20.4 %reduce-scatter.13.cloned.1.call-done = f32[32,384]{1,0:T(8,128)} async-done(((f32[128,384]{1,0:T(8,128)}), f32[32,384]{1,0:T(8,128)}) %reduce-scatter.13.cloned.1.call-update) | async-done | bytes 49168 | tf_op jit(solution)/shard_map/reduce_scatter | solution.py:144
  252.8 21.4 %reduce-scatter.25.cloned.1.call-done = f32[56,384]{1,0:T(8,128)} async-done(((f32[224,384]{1,0:T(8,128)}), f32[56,384]{1,0:T(8,128)}) %reduce-scatter.25.cloned.1.call-update) | async-done | bytes 86032
  274.2 27.4 %reduce-scatter.17.cloned.1.call-done = f32[240,256]{1,0:T(8,128)} async-done(((f32[960,256]{1,0:T(8,128)}), f32[240,256]{1,0:T(8,128)}) %reduce-scatter.17.cloned.1.call-update) | async-done | bytes 245776 | tf_op jit(solution)/shard_map/reduce_scatter | solution.py:145
  (55 shorter events, 0.9 us)
Async XLA Ops:
  7.2 1.5 copy-start.13
  7.2 158.7 %reduce-scatter.19.cloned.1.call-start = ((), (), s32[]{:S(2)}) async-start(), calls=%async_computation.12 | async-start | bytes 983040 | tf_op jit(solution)/shard_map/reduce_scatter | solution.py:140
  10.1 15.7 %copy-start.8 = (bf16[384,896]{1,0:T(8,128)(2,1)S(1)}, bf16[384,896]{1,0:T(8,128)(2,1)}, u32[]{:S(2)}) copy-start(bf16[384,896]{1,0:T(8,128)(2,1)} %param.11) | copy-start | bytes 2064388
  10.6 22.2 %copy-start = (bf16[5,768,256]{2,1,0:T(8,128)(2,1)S(1)}, bf16[5,768,256]{2,1,0:T(8,128)(2,1)}, u32[]{:S(2)}) copy-start(bf16[5,768,256]{2,1,0:T(8,128)(2,1)} %param.9) | copy-start | bytes 5898244
  11.6 47.2 %collective-permute-start.1 = (bf16[1,256,768]{2,1,0:T(8,128)(2,1)}, bf16[1,256,768]{2,1,0:T(8,128)(2,1)}, u32[]{:S(2)}, u32[]{:S(2)}) collective-permute-start(bf16[1,256,768]{2,1,0:T(8,128)(2,1)} %fusion.86), channel_id=1, source_target_pairs={{4,0},{8,4},{12,8},{5,1},{9,5},{13,9},{6,2},{10,6},{14,10},{7,3},{... | collective-permute-start | bytes 1179656 | tf_op jit(solution)/shard_map/ppermute | solution.py:19
  12.8 43.1 %collective-permute-start = (bf16[1,256,768]{2,1,0:T(8,128)(2,1)}, bf16[1,256,768]{2,1,0:T(8,128)(2,1)}, u32[]{:S(2)}, u32[]{:S(2)}) collective-permute-start(bf16[1,256,768]{2,1,0:T(8,128)(2,1)} %fusion.86), channel_id=1, source_target_pairs={{0,4},{4,8},{8,12},{1,5},{5,9},{9,13},{2,6},{6,10},{10,14},{3,7},{... | collective-permute-start | bytes 1179656 | tf_op jit(solution)/shard_map/ppermute | solution.py:18
  54.1 1.8 copy-start.1
  55.5 1.9 copy-start.4
  60.1 2.6 copy-start.14
  60.1 2.6 copy-start.15
  62.7 1.2 copy-start.9
  62.7 1.3 copy-start.10
  62.7 1.7 copy-start.16
  63.1 0.7 copy-start.12
  65.1 1.1 copy-start.11
  65.7 6.1 %copy-start.6 = (bf16[256,768]{1,0:T(8,128)(2,1)}, bf16[256,768]{1,0:T(8,128)(2,1)S(1)}, u32[]{:S(2)}) copy-start(bf16[256,768]{1,0:T(8,128)(2,1)S(1)} %convolution_convert_fusion) | copy-start | bytes 1179652
  66.2 19.1 %collective-permute-start.3 = (bf16[1,256,512]{2,1,0:T(8,128)(2,1)S(1)}, bf16[1,256,512]{2,1,0:T(8,128)(2,1)}, u32[]{:S(2)}, u32[]{:S(2)}) collective-permute-start(bf16[1,256,512]{2,1,0:T(8,128)(2,1)S(1)} %bitcast.109), channel_id=1, source_target_pairs={{0,4},{4,8},{8,12},{1,5},{5,9},{9,13},{2,6},{6,10},{10,14},{3,7},{... | collective-permute-start | bytes 786440 | tf_op jit(solution)/shard_map/ppermute | solution.py:18
  70.1 16.6 %collective-permute-start.2 = (bf16[1,256,512]{2,1,0:T(8,128)(2,1)S(1)}, bf16[1,256,512]{2,1,0:T(8,128)(2,1)}, u32[]{:S(2)}, u32[]{:S(2)}) collective-permute-start(bf16[1,256,512]{2,1,0:T(8,128)(2,1)S(1)} %bitcast.110), channel_id=1, source_target_pairs={{4,0},{8,4},{12,8},{5,1},{9,5},{13,9},{6,2},{10,6},{14,10},{7,3},{... | collective-permute-start | bytes 786440 | tf_op jit(solution)/shard_map/ppermute | solution.py:19
  71.8 1.2 copy-start.5
  83.5 82.9 %reduce-scatter.11.cloned.1.call-start = ((), (), s32[]{:S(2)}) async-start(), calls=%async_computation.8 | async-start | bytes 983040 | tf_op jit(solution)/shard_map/reduce_scatter | solution.py:138
  83.6 3.1 copy-start.2
  89.3 1.5 copy-start.7
  98.2 68.8 %reduce-scatter.23.cloned.1.call-start = ((), (), s32[]{:S(2)}) async-start(), calls=%async_computation.14 | async-start | bytes 1720320 | tf_op jit(solution)/shard_map/reduce_scatter | solution.py:141
  115.7 94.6 %reduce-scatter.15.cloned.1.call-start = ((), (), s32[]{:S(2)}) async-start(), calls=%async_computation.10 | async-start | bytes 4915200 | tf_op jit(solution)/shard_map/reduce_scatter | solution.py:139
  122.1 3.1 copy-start.3
  165.8 66.6 %reduce-scatter.21.cloned.1.call-start = ((), (), s32[]{:S(2)}) async-start(), calls=%async_computation.13 | async-start | bytes 245760 | tf_op jit(solution)/shard_map/reduce_scatter | solution.py:146
  166.4 86.4 %reduce-scatter.13.cloned.1.call-start = ((), (), s32[]{:S(2)}) async-start(), calls=%async_computation.9 | async-start | bytes 245760 | tf_op jit(solution)/shard_map/reduce_scatter | solution.py:144
  167.0 107.2 %reduce-scatter.25.cloned.1.call-start = ((), (), s32[]{:S(2)}) async-start(), calls=%async_computation.15 | async-start | bytes 430080
  167.7 133.8 %reduce-scatter.17.cloned.1.call-start = ((), (), s32[]{:S(2)}) async-start(), calls=%async_computation.11 | async-start | bytes 1228800 | tf_op jit(solution)/shard_map/reduce_scatter | solution.py:145
Sparse Core Ops, SparseCore 0:
  83.7 24.8 reduce-scatter.18
  111.3 23.2 reduce-scatter.10
  137.2 26.9 reduce-scatter.22
  166.8 43.5 reduce-scatter.14
  213.0 19.3 reduce-scatter.20
  235.2 17.5 reduce-scatter.12
  255.7 18.4 reduce-scatter.24
  277.1 24.4 reduce-scatter.16
where the time goes:
time: 313 us; the launch traced here: 308 us
  waiting for transfers between devices  136 us (43%)
  local copies, waits for them, and re-layouts  109 us (35%)
  matrix products  25.7 us (8%)
  between operations  14.6 us (5%)
  starting transfers between devices  13.3 us (4%)
  other arithmetic  10.4 us (3%)
    reduce_scatter x1, waiting for transfers between devices, local(): lax.psum_scatter(conv_moved, 'dp', scatter_dimension=0, tiled=True)  42.6 us
    rev x1, local copies, waits for them, and re-layouts, local(): conv_sum[..., half_h:][::-1, ::-1, ::-1]  32.1 us
    reduce_scatter x1, waiting for transfers between devices, local(): lax.psum_scatter(first[1], 'ctx', scatter_dimension=0, tiled=True)  27.4 us
    unnamed x9, waiting for transfers between devices  23.1 us
    reduce_scatter x1, waiting for transfers between devices, local(): lax.psum_scatter(first[2], 'ctx', scatter_dimension=0, tiled=True)  22.1 us
    rev x1, local copies, waits for them, and re-layouts, expand_weights(): conv_half[::-1, ::-1, ::-1]  21.2 us
    reduce_scatter x1, waiting for transfers between devices, local(): lax.psum_scatter(first[0], 'ctx', scatter_dimension=0, tiled=True)  20.4 us
    rev x1, local copies, waits for them, and re-layouts, local(): head_term = head_sum[:, :half_c] + head_sum[:, half_c:][:, ::-1]  11.9 us
  transfers between devices with their start and end apart: 12, of which 5 were waited for; matrix products, arithmetic and copies ran while one was open for 42% of the time, Pallas kernels for 0%

commit v1 on v0

v1 whole, which is shorter than its diff:
```python
import math

import jax
import jax.numpy as jnp
from jax import lax
from jax.sharding import PartitionSpec as P

DILATION_STEP = 128
BF = jnp.bfloat16
F32 = jnp.float32


def mm(a, b):
    return lax.dot_general(a, b, (((1,), (0,)), ((), ())), preferred_element_type=F32)


def mm_nt(a, b):
    return lax.dot_general(a, b, (((1,), (1,)), ((), ())), preferred_element_type=F32)


def mm_tn(a, b):
    return lax.dot_general(a, b, (((0,), (0,)), ((), ())), preferred_element_type=F32)


def exchange(size):
    row = lax.broadcasted_iota(jnp.int32, (size, size), 0)
    col = lax.broadcasted_iota(jnp.int32, (size, size), 1)
    return jnp.where(row + col == size - 1, 1.0, 0.0).astype(BF)


def onehots(marks):
    bases = marks.shape[1]
    row = lax.broadcasted_iota(jnp.int32, (bases, 4 * bases), 0)
    col = lax.broadcasted_iota(jnp.int32, (bases, 4 * bases), 1)
    spread = jnp.where(row == col // 4, 1.0, 0.0).astype(BF)
    spread_rev = jnp.where(bases - 1 - row == col // 4, 1.0, 0.0).astype(BF)
    base = (lax.broadcasted_iota(jnp.int32, (1, 4 * bases), 1) % 4).astype(F32)
    hot = jnp.where(mm(marks, spread) == base + 1.0, 1.0, 0.0).astype(BF)
    hot_rev = jnp.where(mm(marks, spread_rev) == 4.0 - base, 1.0, 0.0).astype(BF)
    return hot, hot_rev


def embed_rows(hot, hot_rev, stem_both, half_c):
    plain = mm(hot, stem_both).astype(BF)
    other = mm(hot_rev, stem_both).astype(BF)
    ordered = jnp.concatenate([plain[:, :half_c], other[:, half_c:]], axis=1)
    reverse = jnp.concatenate([other[:, :half_c], plain[:, half_c:]], axis=1)
    wide = ordered.astype(F32)
    inv_root = lax.rsqrt(jnp.mean(wide * wide, axis=1, keepdims=True) + 1e-05)
    normed = (wide * inv_root).astype(BF)
    normed_rev = (reverse.astype(F32) * inv_root).astype(BF)
    return ordered, reverse, inv_root, normed, normed_rev


def normal_cdf(values):
    return 0.5 * (1.0 + lax.erf(values * (1.0 / math.sqrt(2.0))))


def normal_pdf(values):
    return jnp.exp(-0.5 * values * values) * (1.0 / math.sqrt(2.0 * math.pi))


def halo(x, width):
    count = lax.axis_size("ctx")
    up = [(i, i + 1) for i in range(count - 1)]
    down = [(j, i) for i, j in up]
    before = lax.ppermute(x[x.shape[0] - width :], "ctx", up)
    after = lax.ppermute(x[:width], "ctx", down)
    return jnp.concatenate([before, x, after], axis=0)


def local(tokens, targets, stem, conv, point, head):
    ctx_count = lax.axis_size("ctx")
    dp_count = lax.axis_size("dp")
    rows = tokens.shape[1]
    taps = conv.shape[0]
    half_c, half_h = stem.shape[1], conv.shape[2]
    width = (taps // 2) * DILATION_STEP
    step = DILATION_STEP
    scale = 1.0 / math.sqrt(rows * ctx_count * dp_count)

    marks = halo((tokens[0] + 1).astype(BF), width)
    flip_c = exchange(half_c)
    flip_h = exchange(half_h)
    stem_both = jnp.concatenate([stem, mm(stem, flip_c).astype(BF)], axis=1)
    conv_low = [mm(flip_c, conv[k, half_c:]).astype(BF) for k in range(taps)]
    point_low = mm(flip_h, point[half_h:]).astype(BF)
    point_a = jnp.concatenate([point[:half_h], point_low], axis=1)
    point_b = jnp.concatenate([point_low, point[:half_h]], axis=1)
    head_both = jnp.concatenate([head, head], axis=0)

    hot, hot_rev = onehots(marks)
    ordered, reverse, inv_root, normed, normed_rev = embed_rows(hot, hot_rev, stem_both, half_c)
    mid = slice(width, width + rows)
    inv = inv_root[mid]
    embed = jnp.concatenate([ordered[mid, :half_c], reverse[mid, :half_c]], axis=1).astype(F32)

    def tap(x, k):
        return x[k * step : k * step + rows]

    pre_a = sum(mm(tap(normed, k), conv[k]) for k in range(taps))
    pre_b = sum(mm(tap(normed_rev, k), conv[taps - 1 - k]) for k in range(taps))
    pre = jnp.concatenate([pre_a, pre_b], axis=1)
    cdf = normal_cdf(pre)
    act = (pre * cdf).astype(BF)
    act_a, act_b = act[:, :half_h], act[:, half_h:]
    after = (embed + mm(act_a, point_a) + mm(act_b, point_b)).astype(BF)
    logits = mm(after, head_both)
    loss_grad = ((jnp.exp(logits) - targets[0].astype(F32)) * scale).astype(BF)
    up = mm_nt(loss_grad, head).astype(BF)
    up_both = jnp.concatenate([up, up], axis=1)
    act_grad = mm_nt(up_both, point_a)
    slope = cdf + pre * normal_pdf(pre)
    pre_grad = (jnp.concatenate([act_grad, act_grad], axis=1) * slope).astype(BF)
    pre_halo = halo(pre_grad, width)

    g_head = mm_tn(
        jnp.concatenate([loss_grad, loss_grad], axis=0),
        jnp.concatenate([after[:, :half_c], after[:, half_c:]], axis=0),
    )
    act_all = jnp.concatenate(
        [
            jnp.concatenate([act_a, mm(act_b, flip_h).astype(BF)], axis=1),
            jnp.concatenate([act_b, mm(act_a, flip_h).astype(BF)], axis=1),
        ],
        axis=0,
    )
    g_point = mm_tn(act_all, jnp.concatenate([up, up], axis=0))
    grads = jnp.concatenate([pre_grad[:, :half_h], pre_grad[:, half_h:]], axis=0)
    g_conv = jnp.concatenate(
        [
            mm_tn(jnp.concatenate([tap(normed, k), tap(normed_rev, taps - 1 - k)], axis=0), grads)
            for k in range(taps)
        ],
        axis=0,
    )
    normed_grad = jnp.zeros((rows, 2 * half_c), F32)
    for k in range(taps):
        piece = tap(pre_halo, taps - 1 - k)
        weight = jnp.concatenate(
            [
                jnp.concatenate([conv[k, :half_c], conv_low[taps - 1 - k]], axis=1),
                jnp.concatenate([conv_low[k], conv[taps - 1 - k, :half_c]], axis=1),
            ],
            axis=0,
        )
        normed_grad = normed_grad + mm_nt(piece, weight)
    inner = jnp.mean(normed_grad * embed, axis=1, keepdims=True)
    embed_grad = (
        inv * normed_grad - embed * inv * inv * inv * inner + up_both.astype(F32)
    ).astype(BF)
    g_stem = mm_tn(
        jnp.concatenate([hot[mid], hot_rev[mid]], axis=0),
        jnp.concatenate([embed_grad[:, :half_c], embed_grad[:, half_c:]], axis=0),
    )

    def reduce(term):
        blocks = term.reshape(ctx_count, dp_count, -1, term.shape[1])
        by_dp = lax.psum_scatter(jnp.swapaxes(blocks, 0, 1), "dp", scatter_dimension=0)
        return lax.psum_scatter(by_dp, "ctx", scatter_dimension=0)

    return reduce(g_stem), reduce(g_conv), reduce(g_point), reduce(g_head)


def solution(mesh):
    return jax.shard_map(
        local,
        mesh=mesh,
        in_specs=(
            P(("groups", "dp"), "ctx", None),
            P(("groups", "dp"), "ctx", None),
            P("groups", None),
            P("groups", None, None),
            P("groups", None),
            P("groups", None),
        ),
        out_specs=(P(("groups", "ctx", "dp"), None),) * 4,
        check_vma=False,
    )
```

time: 313 us -> 275 us (0.88); the launches traced: 308 us -> 274 us
  local copies, waits for them, and re-layouts: 109 us -> 15.5 us
  waiting for transfers between devices: 136 us -> 198 us
  other arithmetic: 10.4 us -> 3.17 us
  matrix products: 25.7 us -> 29 us
    rev x8 -> x0, local copies, waits for them, and re-layouts: 92 us -> none  [the longest x1 32.1 us: local(): conv_sum[..., half_h:][::-1, ::-1, ::-1]]
    reduce_scatter x7, waiting for transfers between devices: 112 us -> 174 us  [the longest x4 104 us: reduce(): lax.psum_scatter(jnp.swapaxes(blocks, 0, 1), 'dp', scatter_dimension=0)]
    add x4 -> x1, other arithmetic: 8 us -> 0.01 us  [onehots(): hot = jnp.where(mm(marks, spread) == base + 1.0, 1.0, 0.0).astype(BF)]
    transpose x4 -> x0, local copies, waits for them, and re-layouts: 5.31 us -> none  [regroup_rows(): return jnp.swapaxes(shaped, 0, 1).reshape(term.shape)]
    reshape x0 -> x4, local copies, waits for them, and re-layouts: none -> 5.25 us  [reduce(): blocks = term.reshape(ctx_count, dp_count, -1, term.shape[1])]
    dot_general x23 -> x41, matrix products: 25.7 us -> 29 us  [the longest x26 17.3 us: mm(): lax.dot_general(a, b, (((1,), (0,)), ((), ())), preferred_element_type=F32)]
    ppermute x4, waiting for transfers between devices: 0.01 us -> 3.2 us  [the longest x2 3.2 us: halo(): after = lax.ppermute(x[:width], 'ctx', down)]
    unnamed x34 -> x50, local copies, waits for them, and re-layouts: 5.57 us -> 7.08 us
  transfers between devices with their start and end apart: 12 -> 12, of which waited for: 5 -> 9; matrix products, arithmetic and copies ran while one was open for 42% -> 12% of each run, Pallas kernels for 0% -> 0%
where the time goes in v1:
time: 275 us; the launch traced here: 274 us
  waiting for transfers between devices  198 us (72%)
  matrix products  29 us (11%)
  local copies, waits for them, and re-layouts  15.5 us (6%)
  between operations  14.8 us (5%)
  starting transfers between devices  13.3 us (5%)
  other arithmetic  3.17 us (1%)
    reduce_scatter x4, waiting for transfers between devices, reduce(): lax.psum_scatter(jnp.swapaxes(blocks, 0, 1), 'dp', scatter_dimension=0)  104 us
    reduce_scatter x3, waiting for transfers between devices, reduce(): return lax.psum_scatter(by_dp, 'ctx', scatter_dimension=0)  69.8 us
    unnamed x9, waiting for transfers between devices  21.5 us
    dot_general x26, matrix products, mm(): lax.dot_general(a, b, (((1,), (0,)), ((), ())), preferred_element_type=F32)  17.3 us
    ppermute x2, starting transfers between devices, halo(): before = lax.ppermute(x[x.shape[0] - width:], 'ctx', up)  10.2 us
    dot_general x7, matrix products, mm_nt(): lax.dot_general(a, b, (((1,), (1,)), ((), ())), preferred_element_type=F32)  8.1 us
    unnamed x50, local copies, waits for them, and re-layouts  7.08 us
  transfers between devices with their start and end apart: 12, of which 9 were waited for; matrix products, arithmetic and copies ran while one was open for 12% of the time, Pallas kernels for 0%

profile of v1, /device:TPU:0, one launch (start us, length us, event | category | flops | bytes accessed | tf_op | source)
XLA Modules:
  0.0 274.0 jit_solution(892306763478106013)
XLA Ops:
  7.2 1.1 fusion.190
  8.3 1.3 collective-permute-start.1
  9.6 6.2 %collective-permute-start = (bf16[256,128]{1,0:T(8,128)(2,1)S(1)}, bf16[256,128]{1,0:T(8,128)(2,1)}, u32[]{:S(2)}, u32[]{:S(2)}) collective-permute-start(bf16[256,128]{1,0:T(8,128)(2,1)S(1)} %fusion.190), channel_id=1, source_target_pairs={{0,4},{4,8},{8,12},{1,5},{5,9},{9,13},{2,6},{6,10},{10,14},{3,7},{... | collective-permute-start | bytes 196616 | tf_op jit(solution)/shard_map/ppermute | solution.py:67
  15.8 1.1 convolution_convert_fusion.8
  16.9 0.9 slice.189
  17.9 1.9 convolution_convert_fusion.5
  19.8 1.0 convolution_convert_fusion.6
  20.9 1.0 convolution_convert_fusion.7
  21.8 1.0 convolution_convert_fusion.4
  22.9 1.0 convolution_convert_fusion.3
  23.9 0.9 copy.28
  24.8 1.2 fusion.21
  26.0 0.9 copy.56
  26.9 0.8 copy.57
  27.7 0.8 copy.55
  28.6 0.8 copy.54
  29.4 0.8 copy.58
  30.2 1.3 select_convert_fusion
  31.5 0.8 convolution_convert_fusion
  32.5 1.2 select_convert_fusion.1
  33.7 0.8 convolution_convert_fusion.1
  35.0 0.5 fusion.1
  35.5 1.0 copy-done.1
  36.8 0.3 convolution_add_fusion.11
  37.2 0.3 convolution_add_fusion.10
  37.5 0.3 convolution_add_fusion.9
  37.8 0.3 convolution_add_fusion.8
  38.5 0.3 convolution_add_fusion.7
  39.1 0.3 convolution_add_fusion.5
  40.8 0.3 fusion.20
  41.1 0.4 copy-done.4
  41.8 0.6 fusion.17
  42.5 0.4 convolution_convert_fusion.9
  43.2 0.9 fusion.91
  44.1 4.0 %collective-permute-start.3 = (bf16[256,512]{0,1:T(8,128)(2,1)}, bf16[256,512]{0,1:T(8,128)(2,1)}, u32[]{:S(2)}, u32[]{:S(2)}) collective-permute-start(bf16[256,512]{0,1:T(8,128)(2,1)} %fusion.91), channel_id=1, source_target_pairs={{0,4},{4,8},{8,12},{1,5},{5,9},{9,13},{2,6},{6,10},{10,14},{3,7},{... | collective-permute-start | bytes 786440 | tf_op jit(solution)/shard_map/ppermute | solution.py:67
  48.1 1.3 collective-permute-start.2
  49.4 0.5 fusion.96
  49.8 0.9 copy.65
  51.1 1.6 fusion.48
  52.8 1.5 fusion.63
  54.3 3.2 %collective-permute-done.2 = bf16[256,512]{0,1:T(8,128)(2,1)} collective-permute-done((bf16[256,512]{0,1:T(8,128)(2,1)}, bf16[256,512]{0,1:T(8,128)(2,1)}, u32[]{:S(2)}, u32[]{:S(2)}) %collective-permute-start.2) | collective-permute-done | bytes 262176 | tf_op jit(solution)/shard_map/ppermute | solution.py:68
  57.5 1.4 fusion.40
  58.9 1.4 fusion.16
  60.4 1.5 fusion.32
  62.2 0.6 slice-done
  62.9 0.5 fusion.92
  63.4 1.0 copy.66
  64.5 0.7 fusion.22
  65.2 1.2 copy.64
  66.5 1.0 fusion.273
  67.8 0.4 convolution_dynamic-update-slice_fusion.4
  68.2 0.4 convolution_dynamic-update-slice_fusion.3
  68.6 0.4 convolution_dynamic-update-slice_fusion.2
  69.0 0.4 convolution_dynamic-update-slice_fusion.1
  69.4 0.4 convolution_dynamic-update-slice_fusion
  69.8 2.1 copy.63
  72.0 3.0 %reduce-scatter.19.cloned.1.call-done = f32[1,4,32,384]{3,2,1,0:T(8,128)} async-done(((f32[4,4,32,384]{3,2,1,0:T(8,128)}), f32[1,4,32,384]{3,2,1,0:T(8,128)}) %reduce-scatter.19.cloned.1.call-update) | async-done | bytes 196624 | tf_op jit(solution)/shard_map/reduce_scatter | solution.py:159
  75.0 26.0 %reduce-scatter.11.cloned.1.call-done = f32[1,4,32,384]{3,2,1,0:T(8,128)} async-done(((f32[4,4,32,384]{3,2,1,0:T(8,128)}), f32[1,4,32,384]{3,2,1,0:T(8,128)}) %reduce-scatter.11.cloned.1.call-update) | async-done | bytes 196624 | tf_op jit(solution)/shard_map/reduce_scatter | solution.py:159
  101.1 29.5 %reduce-scatter.23.cloned.1.call-done = f32[1,4,56,384]{3,2,1,0:T(8,128)} async-done(((f32[4,4,56,384]{3,2,1,0:T(8,128)}), f32[1,4,56,384]{3,2,1,0:T(8,128)}) %reduce-scatter.23.cloned.1.call-update) | async-done | bytes 344080 | tf_op jit(solution)/shard_map/reduce_scatter | solution.py:159
  130.6 45.4 %reduce-scatter.15.cloned.1.call-done = f32[1,4,240,256]{3,2,1,0:T(8,128)} async-done(((f32[4,4,240,256]{3,2,1,0:T(8,128)}), f32[1,4,240,256]{3,2,1,0:T(8,128)}) %reduce-scatter.15.cloned.1.call-update) | async-done | bytes 983056 | tf_op jit(solution)/shard_map/reduce_scatter | solution.py:159
  176.0 22.1 %reduce-scatter.21.cloned.1.call-done = f32[1,32,384]{2,1,0:T(8,128)} async-done(((f32[4,32,384]{2,1,0:T(8,128)}), f32[1,32,384]{2,1,0:T(8,128)}) %reduce-scatter.21.cloned.1.call-update) | async-done | bytes 49168 | tf_op jit(solution)/shard_map/reduce_scatter | solution.py:160
  198.1 20.4 %reduce-scatter.13.cloned.1.call-done = f32[1,32,384]{2,1,0:T(8,128)} async-done(((f32[4,32,384]{2,1,0:T(8,128)}), f32[1,32,384]{2,1,0:T(8,128)}) %reduce-scatter.13.cloned.1.call-update) | async-done | bytes 49168 | tf_op jit(solution)/shard_map/reduce_scatter | solution.py:160
  218.5 21.4 %reduce-scatter.25.cloned.1.call-done = f32[1,56,384]{2,1,0:T(8,128)} async-done(((f32[4,56,384]{2,1,0:T(8,128)}), f32[1,56,384]{2,1,0:T(8,128)}) %reduce-scatter.25.cloned.1.call-update) | async-done | bytes 86032
  239.8 27.3 %reduce-scatter.17.cloned.1.call-done = f32[1,240,256]{2,1,0:T(8,128)} async-done(((f32[4,240,256]{2,1,0:T(8,128)}), f32[1,240,256]{2,1,0:T(8,128)}) %reduce-scatter.17.cloned.1.call-update) | async-done | bytes 245776 | tf_op jit(solution)/shard_map/reduce_scatter | solution.py:160
  (93 shorter events, 4.9 us)
Async XLA Ops:
  7.2 12.7 %copy-start = (bf16[5,768,256]{2,1,0:T(8,128)(2,1)S(1)}, bf16[5,768,256]{2,1,0:T(8,128)(2,1)}, u32[]{:S(2)}) copy-start(bf16[5,768,256]{2,1,0:T(8,128)(2,1)} %param.9) | copy-start | bytes 5898244
  7.2 67.8 %reduce-scatter.19.cloned.1.call-start = ((), (), s32[]{:S(2)}) async-start(), calls=%async_computation.12 | async-start | bytes 983040 | tf_op jit(solution)/shard_map/reduce_scatter | solution.py:159
  8.3 21.9 %collective-permute-start.1 = (bf16[256,128]{1,0:T(8,128)(2,1)S(1)}, bf16[256,128]{1,0:T(8,128)(2,1)S(1)}, u32[]{:S(2)}, u32[]{:S(2)}) collective-permute-start(bf16[256,128]{1,0:T(8,128)(2,1)S(1)} %fusion.190), channel_id=1, source_target_pairs={{4,0},{8,4},{12,8},{5,1},{9,5},{13,9},{6,2},{10,6},{14,10},{7,3},{... | collective-permute-start | bytes 196616 | tf_op jit(solution)/shard_map/ppermute | solution.py:68
  9.6 20.6 %collective-permute-start = (bf16[256,128]{1,0:T(8,128)(2,1)S(1)}, bf16[256,128]{1,0:T(8,128)(2,1)}, u32[]{:S(2)}, u32[]{:S(2)}) collective-permute-start(bf16[256,128]{1,0:T(8,128)(2,1)S(1)} %fusion.190), channel_id=1, source_target_pairs={{0,4},{4,8},{8,12},{1,5},{5,9},{9,13},{2,6},{6,10},{10,14},{3,7},{... | collective-permute-start | bytes 196616 | tf_op jit(solution)/shard_map/ppermute | solution.py:67
  20.9 3.0 %copy-start.7 = (bf16[512,384]{1,0:T(8,128)(2,1)S(1)}, bf16[512,384]{1,0:T(8,128)(2,1)}, u32[]{:S(2)}) copy-start(bf16[512,384]{1,0:T(8,128)(2,1)} %param.8) | copy-start | bytes 1179652
  29.4 2.1 copy-start.8
  29.4 2.1 copy-start.17
  31.5 0.9 copy-start.9
  33.7 0.9 copy-start.10
  35.0 1.5 copy-start.1
  40.4 1.1 copy-start.4
  40.4 1.4 copy-start.16
  42.4 1.6 copy-start.5
  42.9 7.0 %copy-start.2 = (bf16[256,384]{0,1:T(8,128)(2,1)}, bf16[256,384]{0,1:T(8,128)(2,1)S(1)}, u32[]{:S(2)}) copy-start(bf16[256,384]{0,1:T(8,128)(2,1)S(1)} %convolution_convert_fusion.9) | copy-start | bytes 589828
  44.1 8.6 %collective-permute-start.3 = (bf16[256,512]{0,1:T(8,128)(2,1)}, bf16[256,512]{0,1:T(8,128)(2,1)}, u32[]{:S(2)}, u32[]{:S(2)}) collective-permute-start(bf16[256,512]{0,1:T(8,128)(2,1)} %fusion.91), channel_id=1, source_target_pairs={{0,4},{4,8},{8,12},{1,5},{5,9},{9,13},{2,6},{6,10},{10,14},{3,7},{... | collective-permute-start | bytes 786440 | tf_op jit(solution)/shard_map/ppermute | solution.py:67
  48.1 9.4 %collective-permute-start.2 = (bf16[256,512]{0,1:T(8,128)(2,1)}, bf16[256,512]{0,1:T(8,128)(2,1)}, u32[]{:S(2)}, u32[]{:S(2)}) collective-permute-start(bf16[256,512]{0,1:T(8,128)(2,1)} %fusion.91), channel_id=1, source_target_pairs={{4,0},{8,4},{12,8},{5,1},{9,5},{13,9},{6,2},{10,6},{14,10},{7,3},{... | collective-permute-start | bytes 786440 | tf_op jit(solution)/shard_map/ppermute | solution.py:68
  49.8 1.2 copy-start.15
  50.8 50.2 %reduce-scatter.11.cloned.1.call-start = ((), (), s32[]{:S(2)}) async-start(), calls=%async_computation.8 | async-start | bytes 983040 | tf_op jit(solution)/shard_map/reduce_scatter | solution.py:159
  51.0 1.7 copy-start.13
  51.1 1.7 copy-start.14
  51.1 1.7 copy-start.18
  51.1 1.7 copy-start.19
  52.8 4.7 %copy-start.11 = (bf16[1,384,256]{1,2,0:T(8,128)(2,1)S(1)}, bf16[1,384,256]{1,2,0:T(8,128)(2,1)}, u32[]{:S(2)}) copy-start(bf16[1,384,256]{1,2,0:T(8,128)(2,1)} %copy.56) | copy-start | bytes 589828
  52.8 4.7 %copy-start.12 = (bf16[1,384,256]{1,2,0:T(8,128)(2,1)S(1)}, bf16[1,384,256]{1,2,0:T(8,128)(2,1)}, u32[]{:S(2)}) copy-start(bf16[1,384,256]{1,2,0:T(8,128)(2,1)} %copy.57) | copy-start | bytes 589828
  52.8 4.7 %copy-start.20 = (bf16[384,256]{0,1:T(8,128)(2,1)S(1)}, bf16[384,256]{0,1:T(8,128)(2,1)}, u32[]{:S(2)}) copy-start(bf16[384,256]{0,1:T(8,128)(2,1)} %convolution_convert_fusion.5) | copy-start | bytes 589828
  52.8 4.7 %copy-start.21 = (bf16[384,256]{0,1:T(8,128)(2,1)S(1)}, bf16[384,256]{0,1:T(8,128)(2,1)}, u32[]{:S(2)}) copy-start(bf16[384,256]{0,1:T(8,128)(2,1)} %convolution_convert_fusion.4) | copy-start | bytes 589828
  60.4 1.6 copy-start.3
  61.9 1.0 slice-start
  61.9 1.0 slice-start.1
  63.4 1.2 copy-start.6
  64.4 66.1 %reduce-scatter.23.cloned.1.call-start = ((), (), s32[]{:S(2)}) async-start(), calls=%async_computation.14 | async-start | bytes 1720320 | tf_op jit(solution)/shard_map/reduce_scatter | solution.py:159
  66.5 109.5 %reduce-scatter.15.cloned.1.call-start = ((), (), s32[]{:S(2)}) async-start(), calls=%async_computation.10 | async-start | bytes 4915200 | tf_op jit(solution)/shard_map/reduce_scatter | solution.py:159
  71.9 126.1 %reduce-scatter.21.cloned.1.call-start = ((), (), s32[]{:S(2)}) async-start(), calls=%async_computation.13 | async-start | bytes 245760 | tf_op jit(solution)/shard_map/reduce_scatter | solution.py:160
  75.0 143.5 %reduce-scatter.13.cloned.1.call-start = ((), (), s32[]{:S(2)}) async-start(), calls=%async_computation.9 | async-start | bytes 245760 | tf_op jit(solution)/shard_map/reduce_scatter | solution.py:160
  101.0 138.8 %reduce-scatter.25.cloned.1.call-start = ((), (), s32[]{:S(2)}) async-start(), calls=%async_computation.15 | async-start | bytes 430080
  130.6 136.6 %reduce-scatter.17.cloned.1.call-start = ((), (), s32[]{:S(2)}) async-start(), calls=%async_computation.11 | async-start | bytes 1228800 | tf_op jit(solution)/shard_map/reduce_scatter | solution.py:160
Sparse Core Ops, SparseCore 0:
  50.9 23.9 reduce-scatter.18
  77.7 23.2 reduce-scatter.10
  103.5 26.9 reduce-scatter.22
  133.1 42.8 reduce-scatter.14
  178.7 19.3 reduce-scatter.20
  200.8 17.5 reduce-scatter.12
  221.3 18.4 reduce-scatter.24
  242.7 24.3 reduce-scatter.16

commit v2 on v1

--- a/solution.py
+++ b/solution.py
@@ -1,8 +1,11 @@
+import functools
 import math
 
 import jax
 import jax.numpy as jnp
 from jax import lax
+from jax.experimental import pallas as pl
+from jax.experimental.pallas import tpu as pltpu
 from jax.sharding import PartitionSpec as P
 
 DILATION_STEP = 128
@@ -32,9 +35,9 @@
     bases = marks.shape[1]
     row = lax.broadcasted_iota(jnp.int32, (bases, 4 * bases), 0)
     col = lax.broadcasted_iota(jnp.int32, (bases, 4 * bases), 1)
-    spread = jnp.where(row == col // 4, 1.0, 0.0).astype(BF)
-    spread_rev = jnp.where(bases - 1 - row == col // 4, 1.0, 0.0).astype(BF)
-    base = (lax.broadcasted_iota(jnp.int32, (1, 4 * bases), 1) % 4).astype(F32)
+    spread = jnp.where(row == lax.shift_right_logical(col, 2), 1.0, 0.0).astype(BF)
+    spread_rev = jnp.where(bases - 1 - row == lax.shift_right_logical(col, 2), 1.0, 0.0).astype(BF)
+    base = jnp.bitwise_and(lax.broadcasted_iota(jnp.int32, (1, 4 * bases), 1), 3).astype(F32)
     hot = jnp.where(mm(marks, spread) == base + 1.0, 1.0, 0.0).astype(BF)
     hot_rev = jnp.where(mm(marks, spread_rev) == 4.0 - base, 1.0, 0.0).astype(BF)
     return hot, hot_rev
@@ -69,7 +72,7 @@
     return jnp.concatenate([before, x, after], axis=0)
 
 
-def local(tokens, targets, stem, conv, point, head):
+def plain(tokens, targets, stem, conv, point, head):
     ctx_count = lax.axis_size("ctx")
     dp_count = lax.axis_size("dp")
     rows = tokens.shape[1]
@@ -161,6 +164,360 @@
 
     return reduce(g_stem), reduce(g_conv), reduce(g_point), reduce(g_head)
 
+MESH = pl.DeviceIdType.MESH
+
+
+def up16(rows):
+    return -(-rows // 16) * 16
+
+
+def encode(values, out, slot):
+    rows, cols = values.shape
+    largest = jnp.maximum(jnp.max(jnp.abs(values), axis=0, keepdims=True), 1e-30)
+    power = jnp.ceil(jnp.log2(largest))
+    scaled = jnp.clip(jnp.round(values * jnp.exp2(15.0 - power)), -32767.0, 32767.0)
+    out[slot, 0:rows] = scaled.astype(jnp.int32).astype(jnp.int16)
+    tail = jnp.broadcast_to(power, (16, cols)).astype(jnp.int32).astype(jnp.int16)
+    out[slot, up16(rows) : up16(rows) + 16] = tail
+
+
+def decode(ref, slot, rows):
+    values = ref[slot, 0:rows].astype(jnp.int32).astype(F32)
+    power = ref[slot, up16(rows) : up16(rows) + 16].astype(jnp.int32).astype(F32)[0:1]
+    return values * jnp.exp2(power - 15.0)
+
+
+def kernel(ctx_count, dp_count, chunks, *refs):
+    tokens, targets, stem, conv, point, head = refs[:6]
+    o_stem, o_conv, o_point, o_head = refs[6:10]
+    marks, pre_grads, normed, normed_rev, conv_low = refs[10:15]
+    count = len(chunks)
+    grad = refs[15 : 15 + count]
+    from_core = refs[15 + count : 15 + 2 * count]
+    to_x = refs[15 + 2 * count : 15 + 3 * count]
+    from_x = refs[15 + 3 * count : 15 + 4 * count]
+    to_z = refs[15 + 4 * count : 15 + 5 * count]
+    from_z = refs[15 + 5 * count : 15 + 6 * count]
+    (halo_send, halo_recv, core_send, core_recv, x_send, x_recv, z_send, z_recv) = refs[15 + 6 * count :]
+
+    group = lax.axis_index("groups")
+    ctx = lax.axis_index("ctx")
+    dp = lax.axis_index("dp")
+    core = lax.rem(dp, 2)
+    side = dp // 2
+    sibling = (group, ctx, dp + 1 - 2 * core)
+    across = (group, ctx, lax.rem(dp + 2, dp_count))
+
+    def along(distance):
+        return (group, lax.rem(ctx + distance, ctx_count), dp)
+
+    rows = tokens.shape[1]
+    taps = conv.shape[0]
+    half_c, half_h = stem.shape[1], conv.shape[2]
+    width = (taps // 2) * DILATION_STEP
+    step = DILATION_STEP
+    mid = slice(width, width + rows)
+    scale = 1.0 / math.sqrt(rows * ctx_count * dp_count)
+
+    def zero_ends(buffer):
+        zeros = jnp.zeros((width, buffer.shape[1]), buffer.dtype)
+
+        @pl.when(ctx == 0)
+        def _():
+            buffer[0:width] = zeros
+
+        @pl.when(ctx == ctx_count - 1)
+        def _():
+            buffer[width + rows : 2 * width + rows] = zeros
+
+    def halo_copies(buffer, kind):
+        upward = pltpu.make_async_remote_copy(
+            src_ref=buffer.at[rows : rows + width],
+            dst_ref=buffer.at[0:width],
+            send_sem=halo_send.at[2 * kind],
+            recv_sem=halo_recv.at[2 * kind],
+            device_id=along(1),
+            device_id_type=MESH,
+        )
+        downward = pltpu.make_async_remote_copy(
+            src_ref=buffer.at[width : 2 * width],
+            dst_ref=buffer.at[width + rows : 2 * width + rows],
+            send_sem=halo_send.at[2 * kind + 1],
+            recv_sem=halo_recv.at[2 * kind + 1],
+            device_id=along(ctx_count - 1),
+            device_id_type=MESH,
+        )
+        return upward, downward
+
+    def halo_start(buffer, kind):
+        upward, downward = halo_copies(buffer, kind)
+        pl.when(ctx < ctx_count - 1)(upward.start)
+        pl.when(ctx > 0)(downward.start)
+
+    def halo_wait(buffer, kind):
+        upward, downward = halo_copies(buffer, kind)
+        pl.when(ctx > 0)(upward.wait_recv)
+        pl.when(ctx < ctx_count - 1)(downward.wait_recv)
+
+    def halo_sent(buffer, kind):
+        upward, downward = halo_copies(buffer, kind)
+        pl.when(ctx < ctx_count - 1)(upward.wait_send)
+        pl.when(ctx > 0)(downward.wait_send)
+
+    def core_copy(c):
+        return pltpu.make_async_remote_copy(
+            src_ref=grad[c].at[:, 1 - core],
+            dst_ref=from_core[c],
+            send_sem=core_send.at[c],
+            recv_sem=core_recv.at[c],
+            device_id=sibling,
+            device_id_type=MESH,
+        )
+
+    def x_copy(c):
+        return pltpu.make_async_remote_copy(
+            src_ref=to_x[c],
+            dst_ref=from_x[c],
+            send_sem=x_send.at[c],
+            recv_sem=x_recv.at[c],
+            device_id=across,
+            device_id_type=MESH,
+        )
+
+    def z_copy(c, distance):
+        return pltpu.make_async_remote_copy(
+            src_ref=to_z[c].at[distance - 1],
+            dst_ref=from_z[c].at[distance - 1],
+            send_sem=z_send.at[c * (ctx_count - 1) + distance - 1],
+            recv_sem=z_recv.at[c * (ctx_count - 1) + distance - 1],
+            device_id=along(distance),
+            device_id_type=MESH,
+        )
+
+    def x_stage(c):
+        core_copy(c).wait_recv()
+
+        @pl.loop(0, ctx_count)
+        def _(i):
+            n = 2 * i + 1 - side
+            encode(grad[c][n, core] + from_core[c][n], to_x[c], i)
+
+        x_copy(c).start()
+
+    def chip_sum(c, i):
+        n = 2 * i + side
+        return grad[c][n, core] + from_core[c][n] + decode(from_x[c], i, chunks[c][0])
+
+    def z_stage(c):
+        x_copy(c).wait_recv()
+        for distance in range(1, ctx_count):
+            encode(chip_sum(c, lax.rem(ctx + distance, ctx_count)), to_z[c], distance - 1)
+            z_copy(c, distance).start()
+
+    def last_stage(c):
+        total = chip_sum(c, ctx)
+        for distance in range(1, ctx_count):
+            z_copy(c, distance).wait_recv()
+            total = total + decode(from_z[c], distance - 1, chunks[c][0])
+        return total
+
+    marks[mid] = (tokens[0] + 1).astype(F32).astype(BF)
+    zero_ends(marks)
+    zero_ends(pre_grads)
+    barrier = pltpu.get_barrier_semaphore()
+    partners = [sibling, across] + [along(d) for d in range(1, ctx_count)]
+    for partner in partners:
+        pl.semaphore_signal(barrier, inc=1, device_id=partner, device_id_type=MESH)
+    pl.semaphore_wait(barrier, len(partners))
+    halo_start(marks, 0)
+
+    flip_c = exchange(half_c)
+    flip_h = exchange(half_h)
+    stem_both = jnp.concatenate([stem[...], mm(stem[...], flip_c).astype(BF)], axis=1)
+    for k in range(taps):
+        conv_low[k] = mm(flip_c, conv[k, half_c:]).astype(BF)
+    point_high = point[0:half_h]
+    point_low = mm(flip_h, point[half_h:]).astype(BF)
+    point_a = jnp.concatenate([point_high, point_low], axis=1)
+    point_b = jnp.concatenate([point_low, point_high], axis=1)
+
+    def embed_part(start, size):
+        part = slice(start, start + size)
+        hot, hot_rev = onehots(marks[part])
+        ordered, reverse, inv, one, other = embed_rows(hot, hot_rev, stem_both, half_c)
+        normed[part] = one
+        normed_rev[part] = other
+        return hot, hot_rev, ordered, reverse, inv
+
+    hot, hot_rev, ordered, reverse, inv = embed_part(width, rows)
+    embed = jnp.concatenate([ordered[:, :half_c], reverse[:, :half_c]], axis=1).astype(F32)
+    halo_wait(marks, 0)
+    embed_part(0, width)
+    embed_part(width + rows, width)
+
+    def tap(ref, k):
+        return ref[k * step : k * step + rows]
+
+    pre_a = sum(mm(tap(normed, k), conv[k]) for k in range(taps))
+    pre_b = sum(mm(tap(normed_rev, k), conv[taps - 1 - k]) for k in range(taps))
+    pre = jnp.concatenate([pre_a, pre_b], axis=1)
+    cdf = normal_cdf(pre)
+    act = (pre * cdf).astype(BF)
+    slope = cdf + pre * normal_pdf(pre)
+    act_a, act_b = act[:, :half_h], act[:, half_h:]
+    after = (embed + mm(act_a, point_a) + mm(act_b, point_b)).astype(BF)
+    head_both = jnp.concatenate([head[...], head[...]], axis=0)
+    logits = mm(after, head_both)
+    loss_grad = ((jnp.exp(logits) - targets[0].astype(F32)) * scale).astype(BF)
+    up = mm_nt(loss_grad, head[...]).astype(BF)
+    up_both = jnp.concatenate([up, up], axis=1)
+    act_grad = mm_nt(up_both, point_a)
+    pre_grad = (jnp.concatenate([act_grad, act_grad], axis=1) * slope).astype(BF)
+    pre_grads[mid] = pre_grad
+    halo_start(pre_grads, 1)
+
+    blocks = ctx_count * dp_count
+    head_rows, point_rows = o_head.shape[0], o_point.shape[0]
+    g_head = mm_tn(
+        jnp.concatenate([loss_grad, loss_grad], axis=0),
+        jnp.concatenate([after[:, :half_c], after[:, half_c:]], axis=0),
+    )
+    for n in range(blocks):
+        grad[0][n // 2, n % 2, 0:head_rows] = g_head[n * head_rows : (n + 1) * head_rows]
+    act_all = jnp.concatenate(
+        [
+            jnp.concatenate([act_a, mm(act_b, flip_h).astype(BF)], axis=1),
+            jnp.concatenate([act_b, mm(act_a, flip_h).astype(BF)], axis=1),
+        ],
+        axis=0,
+    )
+    g_point = mm_tn(act_all, jnp.concatenate([up, up], axis=0))
+    for n in range(blocks):
+        grad[0][n // 2, n % 2, head_rows : head_rows + point_rows] = g_point[
+            n * point_rows : (n + 1) * point_rows
+        ]
+    core_copy(0).start()
+
+    conv_rows = o_conv.shape[0]
+    conv_cols = chunks[1][1]
+    grads = jnp.concatenate([pre_grad[:, :half_h], pre_grad[:, half_h:]], axis=0)
+    for k in range(taps):
+        both = jnp.concatenate([tap(normed, k), tap(normed_rev, taps - 1 - k)], axis=0)
+        term = mm_tn(both, grads)
+        first, end = k * 2 * half_c, (k + 1) * 2 * half_c
+        at = first
+        while at < end:
+            n = at // conv_rows
+            stop = min(end, (n + 1) * conv_rows)
+            for c in range(half_h // conv_cols):
+                grad[1 + c][n // 2, n % 2, at - n * conv_rows : stop - n * conv_rows] = term[
+                    at - first : stop - first, c * conv_cols : (c + 1) * conv_cols
+                ]
+            at = stop
+    core_copy(1).start()
+    core_copy(2).start()
+    x_stage(0)
+    x_stage(1)
+    x_stage(2)
+
+    halo_wait(pre_grads, 1)
+    normed_grad = jnp.zeros((rows, 2 * half_c), F32)
+    for k in range(taps):
+        weight = jnp.concatenate(
+            [
+                jnp.concatenate([conv[k, 0:half_c], conv_low[taps - 1 - k]], axis=1),
+                jnp.concatenate([conv_low[k], conv[taps - 1 - k, 0:half_c]], axis=1),
+            ],
+            axis=0,
+        )
+        normed_grad = normed_grad + mm_nt(tap(pre_grads, taps - 1 - k), weight)
+    inner = jnp.mean(normed_grad * embed, axis=1, keepdims=True)
+    embed_grad = (
+        inv * normed_grad - embed * inv * inv * inv * inner + up_both.astype(F32)
+    ).astype(BF)
+    g_stem = mm_tn(
+        jnp.concatenate([hot, hot_rev], axis=0),
+        jnp.concatenate([embed_grad[:, :half_c], embed_grad[:, half_c:]], axis=0),
+    )
+    stem_rows = o_stem.shape[0]
+    for n in range(blocks):
+        grad[3][n // 2, n % 2] = g_stem[n * stem_rows : (n + 1) * stem_rows]
+    core_copy(3).start()
+
+    z_stage(0)
+    x_stage(3)
+    z_stage(1)
+    z_stage(2)
+    z_stage(3)
+    total = last_stage(0)
+    o_head[...] = total[0:head_rows]
+    o_point[...] = total[head_rows : head_rows + point_rows]
+    o_conv[:, 0:conv_cols] = last_stage(1)
+    o_conv[:, conv_cols : 2 * conv_cols] = last_stage(2)
+    o_stem[...] = last_stage(3)
+
+    halo_sent(marks, 0)
+    halo_sent(pre_grads, 1)
+    for c in range(count):
+        core_copy(c).wait_send()
+        x_copy(c).wait_send()
+        for distance in range(1, ctx_count):
+            z_copy(c, distance).wait_send()
+
+
+def local(tokens, targets, stem, conv, point, head):
+    ctx_count = lax.axis_size("ctx")
+    dp_count = lax.axis_size("dp")
+    rows = tokens.shape[1]
+    taps = conv.shape[0]
+    half_c, half_h = stem.shape[1], conv.shape[2]
+    width = (taps // 2) * DILATION_STEP
+    blocks = ctx_count * dp_count
+    totals = (stem.shape[0], taps * 2 * half_c, point.shape[0], head.shape[1])
+    fits = all(total % (8 * blocks) == 0 for total in totals)
+    if not (fits and dp_count == 4 and 2 <= ctx_count <= 4 and rows >= width and tokens.shape[0] == 1):
+        return plain(tokens, targets, stem, conv, point, head)
+    out_rows = [total // blocks for total in totals]
+    chunks = (
+        (out_rows[3] + out_rows[2], half_c),
+        (out_rows[1], half_h // 2),
+        (out_rows[1], half_h // 2),
+        (out_rows[0], half_c),
+    )
+    vmem = pl.BlockSpec(memory_space=pltpu.VMEM)
+    scratch = [
+        pltpu.VMEM((rows + 2 * width, tokens.shape[2]), BF),
+        pltpu.VMEM((rows + 2 * width, 2 * half_h), BF),
+        pltpu.VMEM((rows + 2 * width, 2 * half_c), BF),
+        pltpu.VMEM((rows + 2 * width, 2 * half_c), BF),
+        pltpu.VMEM((taps, half_c, half_h), BF),
+    ]
+    scratch += [pltpu.VMEM((blocks // 2, 2, r, c), F32) for r, c in chunks]
+    scratch += [pltpu.VMEM((blocks // 2, r, c), F32) for r, c in chunks]
+    for slots in (ctx_count, ctx_count, ctx_count - 1, ctx_count - 1):
+        scratch += [pltpu.VMEM((slots, up16(r) + 16, c), jnp.int16) for r, c in chunks]
+    dma = pltpu.SemaphoreType.DMA
+    count = len(chunks)
+    scratch += [dma((4,)), dma((4,))]
+    scratch += [dma((count,)) for _ in range(4)]
+    scratch += [dma((count * (ctx_count - 1),)) for _ in range(2)]
+    return pl.pallas_call(
+        functools.partial(kernel, ctx_count, dp_count, chunks),
+        out_shape=(
+            jax.ShapeDtypeStruct((out_rows[0], half_c), F32),
+            jax.ShapeDtypeStruct((out_rows[1], half_h), F32),
+            jax.ShapeDtypeStruct((out_rows[2], half_c), F32),
+            jax.ShapeDtypeStruct((out_rows[3], half_c), F32),
+        ),
+        in_specs=[vmem] * 6,
+        out_specs=(vmem,) * 4,
+        scratch_shapes=scratch,
+        compiler_params=pltpu.CompilerParams(
+            collective_id=0, has_side_effects=True, vmem_limit_bytes=56 * 1024 * 1024
+        ),
+        name="step",
+    )(tokens, targets, stem, conv, point, head)
+
 
 def solution(mesh):
     return jax.shard_map(

time: 275 us -> 58.8 us (0.21)
  waiting for transfers between devices: 198 us -> 0 us
  Pallas kernels: 0 us -> 51.9 us
  matrix products: 29 us -> 0 us
  between operations: 14.8 us -> 0.64 us
  starting transfers between devices: 13.3 us -> 0 us
  local copies, waits for them, and re-layouts: 15.5 us -> 6.02 us
  other arithmetic: 3.17 us -> 0 us
    reduce_scatter x7 -> x0, waiting for transfers between devices: 174 us -> none  [the longest x4 104 us: reduce(): lax.psum_scatter(jnp.swapaxes(blocks, 0, 1), 'dp', scatter_dimension=0)]
    pallas_call x0 -> x1, Pallas kernels: none -> 51.9 us  [local(): pl.pallas_call(functools.partial(kernel, ctx_count, dp_count, chunks), ou...]
    dot_general x41 -> x0, matrix products: 29 us -> none  [the longest x26 17.3 us: mm(): lax.dot_general(a, b, (((1,), (0,)), ((), ())), preferred_element_type=F32)]
    unnamed x9 -> x0, waiting for transfers between devices: 21.5 us -> none
    ppermute x4 -> x0, starting transfers between devices: 12.8 us -> none  [the longest x2 10.2 us: halo(): before = lax.ppermute(x[x.shape[0] - width:], 'ctx', up)]
    reshape x4 -> x0, local copies, waits for them, and re-layouts: 5.25 us -> none  [reduce(): blocks = term.reshape(ctx_count, dp_count, -1, term.shape[1])]
    slice x17 -> x0, local copies, waits for them, and re-layouts: 3.22 us -> none  [the longest x1 0.99 us: local(): pre_grad[:, :half_h]]
    ppermute x4 -> x0, waiting for transfers between devices: 3.2 us -> none  [the longest x2 3.2 us: halo(): after = lax.ppermute(x[:width], 'ctx', down)]
  transfers between devices with their start and end apart: 12 -> 0, of which waited for: 9 -> 0; matrix products, arithmetic and copies ran while one was open for 12% -> 0% of each run, Pallas kernels for 0% -> 0%
where the time goes in v2:
time: 58.8 us; the launch traced here: 58.6 us
  Pallas kernels  51.9 us (88%)
  local copies, waits for them, and re-layouts  6.02 us (10%)
  between operations  0.64 us (1%)
    pallas_call x1, Pallas kernels, local(): pl.pallas_call(functools.partial(kernel, ctx_count, dp_count, chunks), ou...  51.9 us
    unnamed x4, local copies, waits for them, and re-layouts  6.02 us

profile of v2, /device:TPU:0, one launch (start us, length us, event | category | flops | bytes accessed | tf_op | source)
XLA Modules:
  0.0 58.6 jit_solution(15806845291609732998)
XLA Ops:
  0.6 51.9 %step.1 = (f32[32,384]{1,0:T(8,128)}, f32[240,256]{1,0:T(8,128)}, f32[32,384]{1,0:T(8,128)}, f32[56,384]{1,0:T(8,128)}) custom-call(s32[1,256,128]{2,1,0:T(8,128)} %refs_0_.1, s32[1,256,896]{2,1,0:T(8,128)} %refs_1_.1, bf16[512,384]{1,0:T(8,128)(2,1)} %refs_2_.1, bf16[5,768,256]{2,1,0:T(8,128)(2,1)} %refs_3_.1, bf16[512,384]{1,0:T(8,128)(2,1)} %refs_4_.1, ...), custom_call_target="tpu_custom_call" | custom-call | tf_op jit(solution)/shard_map/step/pallas_call | solution.py:504
  52.5 1.4 %copy.14 = f32[32,384]{1,0:T(8,128)} copy(f32[32,384]{1,0:T(8,128)} %get-tuple-element.8) | data formatting | bytes 98304
  54.0 1.7 %copy.15 = f32[240,256]{1,0:T(8,128)} copy(f32[240,256]{1,0:T(8,128)} %get-tuple-element.9) | data formatting | bytes 491520
  55.6 1.4 %copy.16 = f32[32,384]{1,0:T(8,128)} copy(f32[32,384]{1,0:T(8,128)} %get-tuple-element.10) | data formatting | bytes 98304
  57.0 1.5 %copy.17 = f32[56,384]{1,0:T(8,128)} copy(f32[56,384]{1,0:T(8,128)} %get-tuple-element.11) | data formatting | bytes 172032

commit v3 on v2

--- a/solution.py
+++ b/solution.py
@@ -167,24 +167,36 @@
 MESH = pl.DeviceIdType.MESH
 
 
-def up16(rows):
-    return -(-rows // 16) * 16
+def packed_rows(rows, cols):
+    return -(-(cols // 128 * rows + 8) // 16) * 16
 
 
 def encode(values, out, slot):
     rows, cols = values.shape
+    groups = cols // 128
+    tail = packed_rows(rows, cols) - groups * rows
     largest = jnp.maximum(jnp.max(jnp.abs(values), axis=0, keepdims=True), 1e-30)
     power = jnp.ceil(jnp.log2(largest))
     scaled = jnp.clip(jnp.round(values * jnp.exp2(15.0 - power)), -32767.0, 32767.0)
-    out[slot, 0:rows] = scaled.astype(jnp.int32).astype(jnp.int16)
-    tail = jnp.broadcast_to(power, (16, cols)).astype(jnp.int32).astype(jnp.int16)
-    out[slot, up16(rows) : up16(rows) + 16] = tail
-
-
-def decode(ref, slot, rows):
-    values = ref[slot, 0:rows].astype(jnp.int32).astype(F32)
-    power = ref[slot, up16(rows) : up16(rows) + 16].astype(jnp.int32).astype(F32)[0:1]
-    return values * jnp.exp2(power - 15.0)
+    line = lax.broadcasted_iota(jnp.int32, (tail, 128), 0)
+    last = jnp.zeros((tail, 128), F32)
+    pieces = []
+    for g in range(groups):
+        lanes = slice(g * 128, (g + 1) * 128)
+        pieces.append(scaled[:, lanes])
+        last = jnp.where(line == g, power[:, lanes], last)
+    out[slot] = jnp.concatenate(pieces + [last], axis=0).astype(jnp.int32).astype(jnp.int16)
+
+
+def decode(ref, slot, rows, cols):
+    values = ref[slot].astype(jnp.int32).astype(F32)
+    groups = cols // 128
+    last = groups * rows
+    pieces = []
+    for g in range(groups):
+        power = values[last + g : last + g + 1]
+        pieces.append(values[g * rows : (g + 1) * rows] * jnp.exp2(power - 15.0))
+    return pieces[0] if groups == 1 else jnp.concatenate(pieces, axis=1)
 
 
 def kernel(ctx_count, dp_count, chunks, *refs):
@@ -274,12 +286,12 @@
             device_id_type=MESH,
         )
 
-    def x_copy(c):
+    def x_copy(c, slot):
         return pltpu.make_async_remote_copy(
-            src_ref=to_x[c],
-            dst_ref=from_x[c],
-            send_sem=x_send.at[c],
-            recv_sem=x_recv.at[c],
+            src_ref=to_x[c].at[slot],
+            dst_ref=from_x[c].at[slot],
+            send_sem=x_send.at[c * ctx_count + slot],
+            recv_sem=x_recv.at[c * ctx_count + slot],
             device_id=across,
             device_id_type=MESH,
         )
@@ -296,29 +308,29 @@
 
     def x_stage(c):
         core_copy(c).wait_recv()
-
-        @pl.loop(0, ctx_count)
-        def _(i):
-            n = 2 * i + 1 - side
-            encode(grad[c][n, core] + from_core[c][n], to_x[c], i)
-
-        x_copy(c).start()
-
-    def chip_sum(c, i):
-        n = 2 * i + side
-        return grad[c][n, core] + from_core[c][n] + decode(from_x[c], i, chunks[c][0])
+        for slot in range(ctx_count):
+            n = 2 * lax.rem(ctx + 1 + slot, ctx_count) + 1 - side
+            encode(grad[c][n, core] + from_core[c][n], to_x[c], slot)
+            x_copy(c, slot).start()
+
+    def chip_sum(c, slot):
+        x_copy(c, slot).wait_recv()
+        n = 2 * lax.rem(ctx + 1 + slot, ctx_count) + side
+        return grad[c][n, core] + from_core[c][n] + decode(from_x[c], slot, *chunks[c])
+
+    def z_part(c, distance):
+        encode(chip_sum(c, distance - 1), to_z[c], distance - 1)
+        z_copy(c, distance).start()
 
     def z_stage(c):
-        x_copy(c).wait_recv()
         for distance in range(1, ctx_count):
-            encode(chip_sum(c, lax.rem(ctx + distance, ctx_count)), to_z[c], distance - 1)
-            z_copy(c, distance).start()
+            z_part(c, distance)
 
     def last_stage(c):
-        total = chip_sum(c, ctx)
+        total = chip_sum(c, ctx_count - 1)
         for distance in range(1, ctx_count):
             z_copy(c, distance).wait_recv()
-            total = total + decode(from_z[c], distance - 1, chunks[c][0])
+            total = total + decode(from_z[c], distance - 1, *chunks[c])
         return total
 
     marks[mid] = (tokens[0] + 1).astype(F32).astype(BF)
@@ -370,12 +382,6 @@
     logits = mm(after, head_both)
     loss_grad = ((jnp.exp(logits) - targets[0].astype(F32)) * scale).astype(BF)
     up = mm_nt(loss_grad, head[...]).astype(BF)
-    up_both = jnp.concatenate([up, up], axis=1)
-    act_grad = mm_nt(up_both, point_a)
-    pre_grad = (jnp.concatenate([act_grad, act_grad], axis=1) * slope).astype(BF)
-    pre_grads[mid] = pre_grad
-    halo_start(pre_grads, 1)
-
     blocks = ctx_count * dp_count
     head_rows, point_rows = o_head.shape[0], o_point.shape[0]
     g_head = mm_tn(
@@ -398,10 +404,18 @@
         ]
     core_copy(0).start()
 
+    up_both = jnp.concatenate([up, up], axis=1)
+    act_grad = mm_nt(up_both, point_a)
+    pre_grad = (jnp.concatenate([act_grad, act_grad], axis=1) * slope).astype(BF)
+    pre_grads[mid] = pre_grad
+    halo_start(pre_grads, 1)
+
     conv_rows = o_conv.shape[0]
     conv_cols = chunks[1][1]
     grads = jnp.concatenate([pre_grad[:, :half_h], pre_grad[:, half_h:]], axis=0)
     for k in range(taps):
+        if k == 2:
+            x_stage(0)
         both = jnp.concatenate([tap(normed, k), tap(normed_rev, taps - 1 - k)], axis=0)
         term = mm_tn(both, grads)
         first, end = k * 2 * half_c, (k + 1) * 2 * half_c
@@ -416,9 +430,9 @@
             at = stop
     core_copy(1).start()
     core_copy(2).start()
-    x_stage(0)
+    for distance in range(1, ctx_count - 1):
+        z_part(0, distance)
     x_stage(1)
-    x_stage(2)
 
     halo_wait(pre_grads, 1)
     normed_grad = jnp.zeros((rows, 2 * half_c), F32)
@@ -444,9 +458,10 @@
         grad[3][n // 2, n % 2] = g_stem[n * stem_rows : (n + 1) * stem_rows]
     core_copy(3).start()
 
-    z_stage(0)
+    z_part(0, ctx_count - 1)
+    x_stage(2)
+    z_stage(1)
     x_stage(3)
-    z_stage(1)
     z_stage(2)
     z_stage(3)
     total = last_stage(0)
@@ -460,9 +475,18 @@
     halo_sent(pre_grads, 1)
     for c in range(count):
         core_copy(c).wait_send()
-        x_copy(c).wait_send()
+        for slot in range(ctx_count):
+            x_copy(c, slot).wait_send()
         for distance in range(1, ctx_count):
             z_copy(c, distance).wait_send()
+
+
+def hand_out(*refs):
+    copies = [pltpu.make_async_copy(refs[i], refs[4 + i], refs[8].at[i]) for i in range(4)]
+    for copy in copies:
+        copy.start()
+    for copy in copies:
+        copy.wait()
 
 
 def local(tokens, targets, stem, conv, point, head):
@@ -495,13 +519,14 @@
     scratch += [pltpu.VMEM((blocks // 2, 2, r, c), F32) for r, c in chunks]
     scratch += [pltpu.VMEM((blocks // 2, r, c), F32) for r, c in chunks]
     for slots in (ctx_count, ctx_count, ctx_count - 1, ctx_count - 1):
-        scratch += [pltpu.VMEM((slots, up16(r) + 16, c), jnp.int16) for r, c in chunks]
+        scratch += [pltpu.VMEM((slots, packed_rows(r, c), 128), jnp.int16) for r, c in chunks]
     dma = pltpu.SemaphoreType.DMA
     count = len(chunks)
     scratch += [dma((4,)), dma((4,))]
-    scratch += [dma((count,)) for _ in range(4)]
+    scratch += [dma((count,)), dma((count,))]
+    scratch += [dma((count * ctx_count,)) for _ in range(2)]
     scratch += [dma((count * (ctx_count - 1),)) for _ in range(2)]
-    return pl.pallas_call(
+    sums = pl.pallas_call(
         functools.partial(kernel, ctx_count, dp_count, chunks),
         out_shape=(
             jax.ShapeDtypeStruct((out_rows[0], half_c), F32),
@@ -517,6 +542,15 @@
         ),
         name="step",
     )(tokens, targets, stem, conv, point, head)
+    anywhere = pl.BlockSpec(memory_space=pl.ANY)
+    return pl.pallas_call(
+        hand_out,
+        out_shape=tuple(jax.ShapeDtypeStruct(x.shape, x.dtype) for x in sums),
+        in_specs=[anywhere] * 4,
+        out_specs=(anywhere,) * 4,
+        scratch_shapes=[dma((4,))],
+        name="hand_out",
+    )(*sums)
 
 
 def solution(mesh):

time: 58.8 us -> 58.2 us (0.990)
  local copies, waits for them, and re-layouts: 6.02 us -> 0 us
  Pallas kernels: 51.9 us -> 57.4 us
    pallas_call x0 -> x1, Pallas kernels: none -> 14.2 us  [local(): pl.pallas_call(hand_out, out_shape=tuple((jax.ShapeDtypeStruct(x.shape, x...]
    pallas_call x1, Pallas kernels: 51.9 us -> 43.3 us  [local(): pl.pallas_call(functools.partial(kernel, ctx_count, dp_count, chunks), ou...]
    unnamed x4 -> x0, local copies, waits for them, and re-layouts: 6.02 us -> none
where the time goes in v3:
time: 58.2 us; the launch traced here: 58.1 us
  Pallas kernels  57.4 us (99%)
  between operations  0.64 us (1%)
    pallas_call x1, Pallas kernels, local(): pl.pallas_call(functools.partial(kernel, ctx_count, dp_count, chunks), ou...  43.3 us
    pallas_call x1, Pallas kernels, local(): pl.pallas_call(hand_out, out_shape=tuple((jax.ShapeDtypeStruct(x.shape, x...  14.2 us

profile of v3, /device:TPU:0, one launch (start us, length us, event | category | flops | bytes accessed | tf_op | source)
XLA Modules:
  0.0 58.1 jit_solution(3282558813642278485)
XLA Ops:
  0.6 43.3 %step.1 = (f32[32,384]{1,0:T(8,128)}, f32[240,256]{1,0:T(8,128)}, f32[32,384]{1,0:T(8,128)}, f32[56,384]{1,0:T(8,128)}) custom-call(s32[1,256,128]{2,1,0:T(8,128)} %refs_0_.1, s32[1,256,896]{2,1,0:T(8,128)} %refs_1_.1, bf16[512,384]{1,0:T(8,128)(2,1)} %refs_2_.1, bf16[5,768,256]{2,1,0:T(8,128)(2,1)} %refs_3_.1, bf16[512,384]{1,0:T(8,128)(2,1)} %refs_4_.1, ...), custom_call_target="tpu_custom_call" | custom-call | tf_op jit(solution)/shard_map/step/pallas_call | solution.py:529
  43.9 14.2 %hand_out.1 = (f32[32,384]{1,0:T(8,128)}, f32[240,256]{1,0:T(8,128)}, f32[32,384]{1,0:T(8,128)}, f32[56,384]{1,0:T(8,128)}) custom-call(f32[32,384]{1,0:T(8,128)} %get-tuple-element.8.refs_0_, f32[240,256]{1,0:T(8,128)} %get-tuple-element.9.refs_1_, f32[32,384]{1,0:T(8,128)} %get-tuple-element.10.refs_2_, f32[56,384]{1,0:T(8,128)} %get-tuple-element.11.refs_3_), custom_call_target="tpu_custom_call" | custom-call | tf_op jit(solution)/shard_map/hand_out/pallas_call | solution.py:546

commit v4 on v3

--- a/solution.py
+++ b/solution.py
@@ -200,8 +200,12 @@
 
 
 def kernel(ctx_count, dp_count, chunks, *refs):
-    tokens, targets, stem, conv, point, head = refs[:6]
-    o_stem, o_conv, o_point, o_head = refs[6:10]
+    in_sems, out_sems = refs[-2:]
+    tokens, targets, stem, conv, point, head = refs[-12:-6]
+    o_stem, o_conv, o_point, o_head = refs[-6:-2]
+    loads = [pltpu.make_async_copy(refs[i], refs[i - 12], in_sems.at[i]) for i in range(6)]
+    stores = [pltpu.make_async_copy(refs[i - 6], refs[i + 6], out_sems.at[i]) for i in range(4)]
+    refs = refs[:-12]
     marks, pre_grads, normed, normed_rev, conv_low = refs[10:15]
     count = len(chunks)
     grad = refs[15 : 15 + count]
@@ -333,25 +337,23 @@
             total = total + decode(from_z[c], distance - 1, *chunks[c])
         return total
 
-    marks[mid] = (tokens[0] + 1).astype(F32).astype(BF)
-    zero_ends(marks)
-    zero_ends(pre_grads)
     barrier = pltpu.get_barrier_semaphore()
     partners = [sibling, across] + [along(d) for d in range(1, ctx_count)]
     for partner in partners:
         pl.semaphore_signal(barrier, inc=1, device_id=partner, device_id_type=MESH)
+    for i in (0, 2, 3, 4, 5, 1):
+        loads[i].start()
+    zero_ends(marks)
+    zero_ends(pre_grads)
+    loads[0].wait()
+    marks[mid] = (tokens[0] + 1).astype(F32).astype(BF)
     pl.semaphore_wait(barrier, len(partners))
     halo_start(marks, 0)
 
     flip_c = exchange(half_c)
     flip_h = exchange(half_h)
+    loads[2].wait()
     stem_both = jnp.concatenate([stem[...], mm(stem[...], flip_c).astype(BF)], axis=1)
-    for k in range(taps):
-        conv_low[k] = mm(flip_c, conv[k, half_c:]).astype(BF)
-    point_high = point[0:half_h]
-    point_low = mm(flip_h, point[half_h:]).astype(BF)
-    point_a = jnp.concatenate([point_high, point_low], axis=1)
-    point_b = jnp.concatenate([point_low, point_high], axis=1)
 
     def embed_part(start, size):
         part = slice(start, start + size)
@@ -363,6 +365,14 @@
 
     hot, hot_rev, ordered, reverse, inv = embed_part(width, rows)
     embed = jnp.concatenate([ordered[:, :half_c], reverse[:, :half_c]], axis=1).astype(F32)
+    loads[3].wait()
+    for k in range(taps):
+        conv_low[k] = mm(flip_c, conv[k, half_c:]).astype(BF)
+    loads[4].wait()
+    point_high = point[0:half_h]
+    point_low = mm(flip_h, point[half_h:]).astype(BF)
+    point_a = jnp.concatenate([point_high, point_low], axis=1)
+    point_b = jnp.concatenate([point_low, point_high], axis=1)
     halo_wait(marks, 0)
     embed_part(0, width)
     embed_part(width + rows, width)
@@ -378,6 +388,8 @@
     slope = cdf + pre * normal_pdf(pre)
     act_a, act_b = act[:, :half_h], act[:, half_h:]
     after = (embed + mm(act_a, point_a) + mm(act_b, point_b)).astype(BF)
+    loads[5].wait()
+    loads[1].wait()
     head_both = jnp.concatenate([head[...], head[...]], axis=0)
     logits = mm(after, head_both)
     loss_grad = ((jnp.exp(logits) - targets[0].astype(F32)) * scale).astype(BF)
@@ -467,12 +479,18 @@
     total = last_stage(0)
     o_head[...] = total[0:head_rows]
     o_point[...] = total[head_rows : head_rows + point_rows]
+    stores[3].start()
+    stores[2].start()
     o_conv[:, 0:conv_cols] = last_stage(1)
     o_conv[:, conv_cols : 2 * conv_cols] = last_stage(2)
+    stores[1].start()
     o_stem[...] = last_stage(3)
+    stores[0].start()
 
     halo_sent(marks, 0)
     halo_sent(pre_grads, 1)
+    for store in stores:
+        store.wait()
     for c in range(count):
         core_copy(c).wait_send()
         for slot in range(ctx_count):
@@ -482,10 +500,15 @@
 
 
 def hand_out(*refs):
-    copies = [pltpu.make_async_copy(refs[i], refs[4 + i], refs[8].at[i]) for i in range(4)]
-    for copy in copies:
+    held, sems = refs[8:12], refs[12]
+    arrive = [pltpu.make_async_copy(refs[i], held[i], sems.at[i]) for i in range(4)]
+    leave = [pltpu.make_async_copy(held[i], refs[4 + i], sems.at[4 + i]) for i in range(4)]
+    for copy in arrive:
         copy.start()
-    for copy in copies:
+    for i in range(4):
+        arrive[i].wait()
+        leave[i].start()
+    for copy in leave:
         copy.wait()
 
 
@@ -508,7 +531,8 @@
         (out_rows[1], half_h // 2),
         (out_rows[0], half_c),
     )
-    vmem = pl.BlockSpec(memory_space=pltpu.VMEM)
+    arguments = (tokens, targets, stem, conv, point, head)
+    anywhere = pl.BlockSpec(memory_space=pl.ANY)
     scratch = [
         pltpu.VMEM((rows + 2 * width, tokens.shape[2]), BF),
         pltpu.VMEM((rows + 2 * width, 2 * half_h), BF),
@@ -526,29 +550,31 @@
     scratch += [dma((count,)), dma((count,))]
     scratch += [dma((count * ctx_count,)) for _ in range(2)]
     scratch += [dma((count * (ctx_count - 1),)) for _ in range(2)]
+    outs = (
+        jax.ShapeDtypeStruct((out_rows[0], half_c), F32),
+        jax.ShapeDtypeStruct((out_rows[1], half_h), F32),
+        jax.ShapeDtypeStruct((out_rows[2], half_c), F32),
+        jax.ShapeDtypeStruct((out_rows[3], half_c), F32),
+    )
+    held = [pltpu.VMEM(x.shape, F32) for x in outs]
+    scratch += [pltpu.VMEM(x.shape, x.dtype) for x in arguments] + held + [dma((6,)), dma((4,))]
     sums = pl.pallas_call(
         functools.partial(kernel, ctx_count, dp_count, chunks),
-        out_shape=(
-            jax.ShapeDtypeStruct((out_rows[0], half_c), F32),
-            jax.ShapeDtypeStruct((out_rows[1], half_h), F32),
-            jax.ShapeDtypeStruct((out_rows[2], half_c), F32),
-            jax.ShapeDtypeStruct((out_rows[3], half_c), F32),
-        ),
-        in_specs=[vmem] * 6,
-        out_specs=(vmem,) * 4,
+        out_shape=outs,
+        in_specs=[anywhere] * 6,
+        out_specs=(anywhere,) * 4,
         scratch_shapes=scratch,
         compiler_params=pltpu.CompilerParams(
             collective_id=0, has_side_effects=True, vmem_limit_bytes=56 * 1024 * 1024
         ),
         name="step",
-    )(tokens, targets, stem, conv, point, head)
-    anywhere = pl.BlockSpec(memory_space=pl.ANY)
+    )(*arguments)
     return pl.pallas_call(
         hand_out,
-        out_shape=tuple(jax.ShapeDtypeStruct(x.shape, x.dtype) for x in sums),
+        out_shape=outs,
         in_specs=[anywhere] * 4,
         out_specs=(anywhere,) * 4,
-        scratch_shapes=[dma((4,))],
+        scratch_shapes=held + [dma((8,))],
         name="hand_out",
     )(*sums)
 

time: 58.2 us -> 43.8 us (0.75)
  Pallas kernels: 57.4 us -> 43 us
    pallas_call x1, Pallas kernels: 14.2 us -> 1.78 us  [local(): pl.pallas_call(hand_out, out_shape=outs, in_specs=[anywhere] * 4, out_spe...]
    pallas_call x1, Pallas kernels: 43.3 us -> 41.3 us  [local(): pl.pallas_call(functools.partial(kernel, ctx_count, dp_count, chunks), ou...]
where the time goes in v4:
time: 43.8 us; the launch traced here: 43.7 us
  Pallas kernels  43 us (98%)
  between operations  0.64 us (1%)
    pallas_call x1, Pallas kernels, local(): pl.pallas_call(functools.partial(kernel, ctx_count, dp_count, chunks), ou...  41.3 us
    pallas_call x1, Pallas kernels, local(): pl.pallas_call(hand_out, out_shape=outs, in_specs=[anywhere] * 4, out_spe...  1.78 us

profile of v4, /device:TPU:0, one launch (start us, length us, event | category | flops | bytes accessed | tf_op | source)
XLA Modules:
  0.0 43.7 jit_solution(2480267124651374662)
XLA Ops:
  0.6 41.3 %step.1 = (f32[32,384]{1,0:T(8,128)}, f32[240,256]{1,0:T(8,128)}, f32[32,384]{1,0:T(8,128)}, f32[56,384]{1,0:T(8,128)}) custom-call(s32[1,256,128]{2,1,0:T(8,128)} %refs_0_.1, s32[1,256,896]{2,1,0:T(8,128)} %refs_1_.1, bf16[512,384]{1,0:T(8,128)(2,1)} %refs_2_.1, bf16[5,768,256]{2,1,0:T(8,128)(2,1)} %refs_3_.1, bf16[512,384]{1,0:T(8,128)(2,1)} %refs_4_.1, ...), custom_call_target="tpu_custom_call" | custom-call | tf_op jit(solution)/shard_map/step/pallas_call | solution.py:561
  41.9 1.8 %hand_out.1 = (f32[32,384]{1,0:T(8,128)}, f32[240,256]{1,0:T(8,128)}, f32[32,384]{1,0:T(8,128)}, f32[56,384]{1,0:T(8,128)}) custom-call(f32[32,384]{1,0:T(8,128)} %get-tuple-element.8.refs_0_, f32[240,256]{1,0:T(8,128)} %get-tuple-element.9.refs_1_, f32[32,384]{1,0:T(8,128)} %get-tuple-element.10.refs_2_, f32[56,384]{1,0:T(8,128)} %get-tuple-element.11.refs_3_), custom_call_target="tpu_custom_call" | custom-call | tf_op jit(solution)/shard_map/hand_out/pallas_call | solution.py:572

commit v5 on v4

--- a/solution.py
+++ b/solution.py
@@ -445,6 +445,8 @@
     for distance in range(1, ctx_count - 1):
         z_part(0, distance)
     x_stage(1)
+    z_part(0, ctx_count - 1)
+    x_stage(2)
 
     halo_wait(pre_grads, 1)
     normed_grad = jnp.zeros((rows, 2 * half_c), F32)
@@ -470,8 +472,6 @@
         grad[3][n // 2, n % 2] = g_stem[n * stem_rows : (n + 1) * stem_rows]
     core_copy(3).start()
 
-    z_part(0, ctx_count - 1)
-    x_stage(2)
     z_stage(1)
     x_stage(3)
     z_stage(2)

time: 43.8 us -> 43.8 us (level)
  no operation moved by 1% of the time
where the time goes in v5:
time: 43.8 us; the launch traced here: 43.7 us
  Pallas kernels  43 us (98%)
  between operations  0.64 us (1%)
    pallas_call x1, Pallas kernels, local(): pl.pallas_call(functools.partial(kernel, ctx_count, dp_count, chunks), ou...  41.3 us
    pallas_call x1, Pallas kernels, local(): pl.pallas_call(hand_out, out_shape=outs, in_specs=[anywhere] * 4, out_spe...  1.78 us

profile of v5, /device:TPU:0, one launch (start us, length us, event | category | flops | bytes accessed | tf_op | source)
XLA Modules:
  0.0 43.7 jit_solution(3591069407949782774)
XLA Ops:
  0.6 41.3 %step.1 = (f32[32,384]{1,0:T(8,128)}, f32[240,256]{1,0:T(8,128)}, f32[32,384]{1,0:T(8,128)}, f32[56,384]{1,0:T(8,128)}) custom-call(s32[1,256,128]{2,1,0:T(8,128)} %refs_0_.1, s32[1,256,896]{2,1,0:T(8,128)} %refs_1_.1, bf16[512,384]{1,0:T(8,128)(2,1)} %refs_2_.1, bf16[5,768,256]{2,1,0:T(8,128)(2,1)} %refs_3_.1, bf16[512,384]{1,0:T(8,128)(2,1)} %refs_4_.1, ...), custom_call_target="tpu_custom_call" | custom-call | tf_op jit(solution)/shard_map/step/pallas_call | solution.py:561
  41.9 1.8 %hand_out.1 = (f32[32,384]{1,0:T(8,128)}, f32[240,256]{1,0:T(8,128)}, f32[32,384]{1,0:T(8,128)}, f32[56,384]{1,0:T(8,128)}) custom-call(f32[32,384]{1,0:T(8,128)} %get-tuple-element.8.refs_0_, f32[240,256]{1,0:T(8,128)} %get-tuple-element.9.refs_1_, f32[32,384]{1,0:T(8,128)} %get-tuple-element.10.refs_2_, f32[56,384]{1,0:T(8,128)} %get-tuple-element.11.refs_3_), custom_call_target="tpu_custom_call" | custom-call | tf_op jit(solution)/shard_map/hand_out/pallas_call | solution.py:572
